TPU v7x, 512 devices: a whole 4x8x8 slice. The times are simulated.
512 devices in a mesh: rows: 64 (over y, x, z_hi), cols: 8 (over z_lo, core).
Axes of the slice: x: 4, y: 8, z: 8 (z_hi: 2, z_lo: 4; z = z_hi * 4 + z_lo), core: 2. Of those that a mesh axis runs over, the one named last changes fastest.
Arguments:
- cross_kernel: float32 [65536, 1024], P('rows', 'cols'), may hold values from -6 to 6
- factor_panels: float32 [2, 512, 65536], P(None, 'cols', 'rows'), may hold values from -0.25 to 0.25
- block_inverses: float32 [2, 512, 512], P(None, 'cols'), may hold values from -0.5 to 1.5, as said below
Outputs:
- solved: float32 [65536, 1024], P('rows', 'cols')
Inputs may be any that keep to these rules, and one draw needn't show every extreme that they name: `block_inverses`: each block is lower triangular, with diagonal entries from 0.5 to 1.5.
All inputs are finite; a program needn't handle non-finite values.
Results may differ from a plain program's by a relative error of at most 0.000084.
Values sent between devices are 32-bit elements; how exact they have to be, the bound alone decides.
A program may use at most 64 MiB of HBM per device.

v0:
```python
import jax
import jax.numpy as jnp
from jax import lax
from jax.sharding import PartitionSpec as P

highest = lax.Precision.HIGHEST


def spread(array, axis, root):
    mine = lax.axis_index(axis) == root
    return lax.psum(jnp.where(mine, array, jnp.zeros_like(array)), axis)


def contract_rows(left, right):
    return lax.dot_general(
        left, right, (((0,), (0,)), ((), ())), precision=highest, preferred_element_type=jnp.float32
    )


def diagonal_solve(inverse_rows, rhs_block):
    return jnp.dot(
        lax.all_gather(inverse_rows, "cols", axis=0, tiled=True),
        rhs_block,
        precision=highest,
        preferred_element_type=jnp.float32,
    )


def share_block(solved_rows):
    return spread(solved_rows, "rows", 0)


def second_update(factor_rows, solved_rows):
    return contract_rows(lax.all_gather(factor_rows, "cols", axis=0, tiled=True), solved_rows)


def on_device(cross_kernel, factor_panels, block_inverses):
    width = block_inverses.shape[2]
    is_zero = lax.axis_index("rows") == 0
    first_factor = lax.all_gather(factor_panels[0], "cols", axis=0, tiled=True)
    first = share_block(diagonal_solve(block_inverses[0], cross_kernel[:width]))
    fresh = cross_kernel - contract_rows(first_factor, first)
    current = jnp.concatenate([jnp.where(is_zero, first, fresh[:width]), fresh[width:]], axis=0)
    second = share_block(diagonal_solve(block_inverses[1], current[width : 2 * width]))
    fresh = current - second_update(factor_panels[1], second)
    top = jnp.where(is_zero, current[:width], fresh[:width])
    middle = jnp.where(is_zero, second, fresh[width : 2 * width])
    return jnp.concatenate([top, middle, fresh[2 * width :]], axis=0)


def solution(mesh):
    in_specs = (P("rows", "cols"), P(None, "cols", "rows"), P(None, "cols", None))
    out_specs = P("rows", "cols")
    return jax.shard_map(
        on_device, mesh=mesh, in_specs=in_specs, out_specs=out_specs, check_vma=False
    )
```

profile of v0, /device:TPU:2, one launch (start us, length us, event | category | flops | bytes accessed | tf_op | source)
XLA Modules:
  0.0 1782.7 jit_solution(6935677184264947465)
XLA Ops:
  6.5 0.0 copy-start
  6.5 0.0 copy-start.3
  6.5 0.0 all-gather.9.cloned.1.call-start
  6.5 1.8 fusion.22
  8.3 0.0 all-gather.9.cloned.1.call-update
  8.3 0.0 all-reduce.3.cloned.1.call-start
  8.4 46.1 %all-gather.9.cloned.1.call-done = f32[1,512,512]{2,1,0:T(8,128)} async-done(((f32[1,64,512]{2,1,0:T(8,128)}), f32[1,512,512]{2,1,0:T(8,128)}) %all-gather.9.cloned.1.call-update) | async-done | bytes 1048592 | tf_op jit(solution)/shard_map/all_gather | solution.py:22
  54.4 3.0 convolution_select_fusion.1
  57.4 0.0 all-reduce.3.cloned.1.call-update
  57.4 0.0 all-gather.11.cloned.1.call-start
  57.5 0.0 copy-done.3
  57.5 0.8 fusion.21
  58.3 0.0 all-gather.11.cloned.1.call-update
  58.3 0.0 all-gather.13.cloned.1.call-start
  58.4 0.5 all-gather.13.cloned.1.call-update
  58.9 0.0 all-gather.15.cloned.1.call-start
  59.0 0.5 all-gather.15.cloned.1.call-update
  59.5 0.0 all-reduce.5.cloned.1.call-start
  59.5 789.4 %all-reduce.3.cloned.1.call-done = f32[512,128]{1,0:T(8,128)} async-done(((f32[512,128]{1,0:T(8,128)}), f32[512,128]{1,0:T(8,128)}) %all-reduce.3.cloned.1.call-update) | async-done | bytes 262160 | tf_op jit(solution)/shard_map/psum | solution.py:11
  848.9 0.0 copy-start.1
  848.9 40.8 %all-gather.11.cloned.1.call-done = f32[1,512,1024]{2,1,0:T(8,128)} async-done(((f32[1,64,1024]{2,1,0:T(8,128)}), f32[1,512,1024]{2,1,0:T(8,128)}) %all-gather.11.cloned.1.call-update) | async-done | bytes 2097168 | tf_op jit(solution)/shard_map/all_gather | solution.py:40
  889.7 0.0 copy-done
  889.7 5.1 fusion.13
  894.8 36.7 %all-gather.13.cloned.1.call-done = f32[1,512,512]{2,1,0:T(8,128)} async-done(((f32[1,64,512]{2,1,0:T(8,128)}), f32[1,512,512]{2,1,0:T(8,128)}) %all-gather.13.cloned.1.call-update) | async-done | bytes 1048592 | tf_op jit(solution)/shard_map/all_gather | solution.py:22
  931.5 2.9 fusion.16
  934.4 0.0 all-reduce.5.cloned.1.call-update
  934.5 0.0 copy-done.1
  934.5 40.0 %all-gather.15.cloned.1.call-done = f32[1,512,1024]{2,1,0:T(8,128)} async-done(((f32[1,64,1024]{2,1,0:T(8,128)}), f32[1,512,1024]{2,1,0:T(8,128)}) %all-gather.15.cloned.1.call-update) | async-done | bytes 2097168 | tf_op jit(solution)/shard_map/all_gather | solution.py:34
  974.6 795.2 %all-reduce.5.cloned.1.call-done = f32[512,128]{1,0:T(8,128)} async-done(((f32[512,128]{1,0:T(8,128)}), f32[512,128]{1,0:T(8,128)}) %all-reduce.5.cloned.1.call-update) | async-done | bytes 262160 | tf_op jit(solution)/shard_map/psum | solution.py:11
  1769.8 0.0 copy-start.2
  1769.8 5.1 fusion.10
  1774.9 0.0 copy-done.2
  1775.0 0.1 slice_select_fusion.1
  1775.0 0.0 copy-start.4
  1775.0 0.8 copy-done.4
  (2 shorter events, 0.0 us)
Async XLA Ops:
  6.5 883.1 %copy-start = (f32[1024,128]{1,0:T(8,128)S(1)}, f32[1024,128]{1,0:T(8,128)}, u32[]{:S(2)}) copy-start(f32[1024,128]{1,0:T(8,128)} %param.3) | copy-start | bytes 1572868
  6.5 50.9 %copy-start.3 = (f32[2,64,1024]{2,1,0:T(8,128)S(1)}, f32[2,64,1024]{2,1,0:T(8,128)}, u32[]{:S(2)}) copy-start(f32[2,64,1024]{2,1,0:T(8,128)} %param.4) | copy-start | bytes 1572868
  6.5 47.9 %all-gather.9.cloned.1.call-start = ((), (), s32[]{:S(2)}) async-start(), calls=%async_computation.2 | async-start | bytes 1179648 | tf_op jit(solution)/shard_map/all_gather | solution.py:22
  8.3 840.6 %all-reduce.3.cloned.1.call-start = ((), (), s32[]{:S(2)}) async-start(), calls=%async_computation | async-start | bytes 524288 | tf_op jit(solution)/shard_map/psum | solution.py:11
  57.4 832.2 %all-gather.11.cloned.1.call-start = ((), (), s32[]{:S(2)}) async-start(), calls=%async_computation.3 | async-start | bytes 2359296 | tf_op jit(solution)/shard_map/all_gather | solution.py:40
  58.3 873.2 %all-gather.13.cloned.1.call-start = ((), (), s32[]{:S(2)}) async-start(), calls=%async_computation.4 | async-start | bytes 1179648 | tf_op jit(solution)/shard_map/all_gather | solution.py:22
  58.9 915.7 %all-gather.15.cloned.1.call-start = ((), (), s32[]{:S(2)}) async-start(), calls=%async_computation.5 | async-start | bytes 2359296 | tf_op jit(solution)/shard_map/all_gather | solution.py:34
  59.5 1710.3 %all-reduce.5.cloned.1.call-start = ((), (), s32[]{:S(2)}) async-start(), calls=%async_computation.1 | async-start | bytes 524288 | tf_op jit(solution)/shard_map/psum | solution.py:11
  848.9 85.6 %copy-start.1 = (f32[512,128]{1,0:T(8,128)S(1)}, f32[512,128]{1,0:T(8,128)}, u32[]{:S(2)}) copy-start(f32[512,128]{1,0:T(8,128)} %all-reduce.3.cloned.1.call-done) | copy-start | bytes 786436
  1769.8 5.2 copy-start.2
  1775.0 0.8 copy-start.4
Sparse Core Ops, SparseCore 0:
  9.4 44.9 all-gather.8
  57.5 791.3 all-reduce.2
  851.2 38.4 all-gather.10
  891.8 39.6 all-gather.12
  933.6 40.8 all-gather.14
  977.6 792.1 all-reduce.4
where the time goes:
time: 1780 us
  waiting for transfers between devices  1750 us (98%)
    psum x2, waiting for transfers between devices, spread(): return lax.psum(jnp.where(mine, array, jnp.zeros_like(array)), axis)  1580 us
    all_gather x2, waiting for transfers between devices, diagonal_solve(): lax.all_gather(inverse_rows, 'cols', axis=0, tiled=True)  82.8 us
    all_gather x1, waiting for transfers between devices, on_device(): first_factor = lax.all_gather(factor_panels[0], 'cols', axis=0, tiled=True)  40.8 us
    all_gather x1, waiting for transfers between devices, second_update(): lax.all_gather(factor_rows, 'cols', axis=0, tiled=True)  40 us
  transfers between devices with their start and end apart: 6, of which 6 were waited for; matrix products, arithmetic and copies ran while one was open for 0% of the time, Pallas kernels for 0%

commit v1 on v0

v1 whole, which is shorter than its diff:
```python
import functools

import jax
import jax.numpy as jnp
from jax import lax
from jax.experimental import pallas as pl
from jax.experimental.pallas import tpu as pltpu
from jax.sharding import PartitionSpec as P

MESH = pl.DeviceIdType.MESH
HIGHEST = lax.Precision.HIGHEST
PLANE = 32
CHUNK = 16
HELPERS = ((1, 3, 4), (28, 5, 7))


def kernel(b_hbm, f_hbm, inv_hbm, o_ref, bv, fall, invf, fb, xb, loc, ag_s, ag_r, in_s, in_r, fb_s, fb_r, sc_s, sc_r, ex_s, ex_r):
    r, c = lax.axis_index("rows"), lax.axis_index("cols")
    m, zh = r // 2, r % 2
    zl, core = c // 2, c % 2
    sib = zl * 2 + 1 - core
    root = r == 0

    def remote(src, dst, s, rs, row, col):
        return pltpu.make_async_remote_copy(
            src_ref=src, dst_ref=dst, send_sem=s, recv_sem=rs,
            device_id={"rows": row, "cols": col}, device_id_type=MESH)

    def away(d):
        return ((zl + d) % 4) * 2 + core

    def rows_of(col):
        return pl.ds(pl.multiple_of(col * 64, 64), 64)

    mine = rows_of(c)
    get_b = pltpu.make_async_copy(b_hbm, bv, loc.at[0])
    get_f = pltpu.make_async_copy(f_hbm, fall.at[:, mine], loc.at[1])
    get_fb = pltpu.make_async_copy(f_hbm.at[0, :, pl.ds(512, 512)], fb.at[mine], loc.at[1])
    get_inv = pltpu.make_async_copy(inv_hbm, invf.at[:, mine], loc.at[2])
    get_b.start()

    @pl.when(root)
    def _():
        get_fb.start()
        get_inv.start()

    @pl.when(jnp.logical_not(root))
    def _():
        get_f.start()

    barrier = pltpu.get_barrier_semaphore()

    def tell(row, col):
        pl.semaphore_signal(barrier, inc=1, device_id={"rows": row, "cols": col}, device_id_type=MESH)

    tell(r, sib)
    for d in (1, 2, 3):
        tell(r, away(d))

    def tell_plane(j, _):
        tell(((m + j) % PLANE) * 2 + zh, c)
        return 0

    lax.fori_loop(1, PLANE, tell_plane, 0)

    @pl.when(zh == 1)
    def _():
        tell(0, c)

    @pl.when(root)
    def _():
        for p in range(2):
            for d in (1, 2, 3):
                tell(HELPERS[p][d - 1] * 2, ((zl + 4 - d) % 4) * 2 + core)
        pl.semaphore_wait(barrier, 4 + 31 + 32)

    helping = functools.reduce(jnp.logical_or, [r == h * 2 for line in HELPERS for h in line])

    @pl.when(helping)
    def _():
        pl.semaphore_wait(barrier, 4 + 31 + 1)

    @pl.when(jnp.logical_not(jnp.logical_or(root, helping)))
    def _():
        pl.semaphore_wait(barrier, 4 + 31)

    for p in range(2):
        for d in (1, 2, 3):
            @pl.when(r == HELPERS[p][d - 1] * 2)
            def _():
                remote(inv_hbm.at[p], invf.at[p, mine], in_s.at[p, d], in_r.at[p, d], 0, away(d)).start()

    def chunk(x, i):
        return xb.at[x, pl.ds(pl.multiple_of(i * CHUNK, CHUNK), CHUNK)]

    def scatter(x):
        def to_one(i, _):
            remote(chunk(x, i), chunk(x, i), sc_s.at[x, 1], sc_r.at[x], i * 2 + 1, c).start()

            @pl.when(i > 0)
            def _():
                remote(chunk(x, i), chunk(x, i), sc_s.at[x, 0], sc_r.at[x], i * 2, c).start()
            return 0

        lax.fori_loop(0, PLANE, to_one, 0)

    def exchange(x):
        def to_one(j, _):
            peer = ((m + j) % PLANE) * 2 + zh

            @pl.when(peer > 0)
            def _():
                remote(chunk(x, m), chunk(x, m), ex_s.at[x], ex_r.at[x], peer, c).start()
            return 0

        lax.fori_loop(1, PLANE, to_one, 0)

    def first_rows(x, n):
        return xb.at[x, pl.ds(0, n * CHUNK)]

    def blocks_across(value):
        return jnp.concatenate([value[i * 128:(i + 1) * 128].T for i in range(4)], axis=0)

    @pl.when(root)
    def _():
        get_inv.wait()
        get_fb.wait()
        own_inv = [remote(invf.at[p, mine], invf.at[p, mine], in_s.at[p, 0], in_r.at[p, 0], 0, sib) for p in range(2)]
        own_fb = [remote(fb.at[mine], fb.at[mine], fb_s.at[d], fb_r.at[d], 0, sib if d == 0 else away(d)) for d in range(4)]
        for copy in own_inv + own_fb:
            copy.start()
        relays = []

        def relay(ref_of, s, rs, arrive_s, arrive_r):
            for d in (1, 2, 3):
                got = ref_of(rows_of(away(4 - d)))
                remote(got, got, arrive_s.at[d], arrive_r.at[d], 0, sib).wait_recv()
                on = remote(got, got, s.at[d + 3], rs.at[d + 3], 0, sib)
                on.start()
                relays.append(on)

        for p in range(2):
            relay(lambda rows: invf.at[p, rows], in_s.at[p], in_r.at[p], in_s.at[p], in_r.at[p])
        own_inv[0].wait_recv()
        for copy in relays[:3]:
            copy.wait_recv()
        get_b.wait()
        first = jnp.dot(invf[0], bv[0:512], precision=HIGHEST, preferred_element_type=jnp.float32)
        o_ref[0:512] = first
        xb[0] = blocks_across(first)
        scatter(0)
        exchange(0)
        relay(lambda rows: fb.at[rows], fb_s, fb_r, fb_s, fb_r)
        own_fb[0].wait_recv()
        for copy in relays[6:]:
            copy.wait_recv()
        rest = bv[512:1024] - lax.dot_general(
            fb[...], o_ref[0:512], (((0,), (0,)), ((), ())), precision=HIGHEST, preferred_element_type=jnp.float32)
        own_inv[1].wait_recv()
        for copy in relays[3:6]:
            copy.wait_recv()
        second = jnp.dot(invf[1], rest, precision=HIGHEST, preferred_element_type=jnp.float32)
        o_ref[512:1024] = second
        xb[1] = blocks_across(second)
        scatter(1)
        exchange(1)
        for copy in own_inv + own_fb + relays:
            copy.wait_send()
        for x in range(2):
            remote(first_rows(x, 31), first_rows(x, 31), sc_s.at[x, 0], sc_r.at[x], 1, c).wait_send()
            remote(first_rows(x, 32), first_rows(x, 32), sc_s.at[x, 1], sc_r.at[x], 1, c).wait_send()
            remote(first_rows(x, 31), first_rows(x, 31), ex_s.at[x], ex_r.at[x], 1, c).wait_send()

    @pl.when(jnp.logical_not(root))
    def _():
        get_f.wait()
        own = [remote(fall.at[:, mine], fall.at[:, mine], ag_s.at[d], ag_r.at[d], r, sib if d == 0 else away(d)) for d in range(4)]
        for copy in own:
            copy.start()
        for x in range(2):
            remote(chunk(x, m), chunk(x, m), sc_s.at[x, 0], sc_r.at[x], 0, c).wait_recv()
            exchange(x)
        relays = []
        for d in (1, 2, 3):
            own[d].wait_recv()
            got = fall.at[:, rows_of(away(4 - d))]
            on = remote(got, got, ag_s.at[d + 3], ag_r.at[d + 3], r, sib)
            on.start()
            relays.append(on)
        own[0].wait_recv()
        for copy in relays:
            copy.wait_recv()
        get_b.wait()
        for x in range(2):
            remote(first_rows(x, 31), first_rows(x, 31), ex_s.at[x], ex_r.at[x], 0, c).wait_recv()
            left = jnp.concatenate([xb[x, i * 128:(i + 1) * 128] for i in range(4)], axis=1)
            src = bv if x == 0 else o_ref

            def update(i, _):
                cut = pl.ds(pl.multiple_of(i * 256, 256), 256)
                took = jnp.dot(left, fall[x, :, cut], precision=HIGHEST, preferred_element_type=jnp.float32)
                o_ref[cut] = src[cut] - took.T
                return 0

            lax.fori_loop(0, 4, update, 0)
        for copy in own + relays:
            copy.wait_send()
        for p in range(2):
            for d in (1, 2, 3):
                @pl.when(r == HELPERS[p][d - 1] * 2)
                def _():
                    remote(inv_hbm.at[p], invf.at[p, mine], in_s.at[p, d], in_r.at[p, d], 0, away(d)).wait_send()
        for x in range(2):
            @pl.when(zh == 0)
            def _():
                remote(first_rows(x, 30), first_rows(x, 30), ex_s.at[x], ex_r.at[x], 1, c).wait_send()

            @pl.when(zh == 1)
            def _():
                remote(first_rows(x, 31), first_rows(x, 31), ex_s.at[x], ex_r.at[x], 1, c).wait_send()


def on_device(cross_kernel, factor_panels, block_inverses):
    dma = pltpu.SemaphoreType.DMA
    any_space = pl.BlockSpec(memory_space=pl.ANY)
    return pl.pallas_call(
        kernel,
        out_shape=jax.ShapeDtypeStruct(cross_kernel.shape, jnp.float32),
        in_specs=[any_space] * 3,
        out_specs=pl.BlockSpec(memory_space=pltpu.VMEM),
        scratch_shapes=[
            pltpu.VMEM((1024, 128), jnp.float32),
            pltpu.VMEM((2, 512, 1024), jnp.float32),
            pltpu.VMEM((2, 512, 512), jnp.float32),
            pltpu.VMEM((512, 512), jnp.float32),
            pltpu.VMEM((2, 512, 128), jnp.float32),
            dma((3,)),
            dma((7,)), dma((7,)),
            dma((2, 7)), dma((2, 7)),
            dma((7,)), dma((7,)),
            dma((2, 2)), dma((2,)),
            dma((2,)), dma((2,)),
        ],
        compiler_params=pltpu.CompilerParams(
            collective_id=0, has_side_effects=True, vmem_limit_bytes=48 << 20),
    )(cross_kernel, factor_panels, block_inverses)


def solution(mesh):
    in_specs = (P("rows", "cols"), P(None, "cols", "rows"), P(None, "cols", None))
    out_specs = P("rows", "cols")
    return jax.shard_map(
        on_device, mesh=mesh, in_specs=in_specs, out_specs=out_specs, check_vma=False
    )
```

time: 1780 us -> 86.2 us (0.05)
  waiting for transfers between devices: 1750 us -> 0 us
  Pallas kernels: 0 us -> 82 us
    psum x2 -> x0, waiting for transfers between devices: 1580 us -> none  [spread(): return lax.psum(jnp.where(mine, array, jnp.zeros_like(array)), axis)]
    all_gather x4 -> x0, waiting for transfers between devices: 164 us -> none  [the longest x2 82.8 us: diagonal_solve(): lax.all_gather(inverse_rows, 'cols', axis=0, tiled=True)]
    pallas_call x0 -> x1, Pallas kernels: none -> 82 us  [on_device(): pl.pallas_call(kernel, out_shape=jax.ShapeDtypeStruct(cross_kernel.shape,...]
  transfers between devices with their start and end apart: 6 -> 0, of which waited for: 6 -> 0; matrix products, arithmetic and copies ran while one was open for 0% -> 0% of each run, Pallas kernels for 0% -> 0%
where the time goes in v1:
time: 86.2 us; the launch traced here: 85.8 us
  Pallas kernels  82 us (95%)
  local copies, waits for them, and re-layouts  3.83 us (4%)
    pallas_call x1, Pallas kernels, on_device(): pl.pallas_call(kernel, out_shape=jax.ShapeDtypeStruct(cross_kernel.shape,...  82 us
    unnamed x7, local copies, waits for them, and re-layouts  3.83 us

profile of v1, /device:TPU:2, one launch (start us, length us, event | category | flops | bytes accessed | tf_op | source)
XLA Modules:
  0.0 85.8 jit_solution(4760703095396062426)
XLA Ops:
  0.0 0.0 copy-start
  0.0 1.0 %copy-done = f32[1024,128]{1,0:T(8,128)S(1)} copy-done((f32[1024,128]{1,0:T(8,128)S(1)}, f32[1024,128]{1,0:T(8,128)}, u32[]{:S(2)}) %copy-start) | copy-done | bytes 524312
  1.0 0.0 copy-start.1
  1.0 1.0 %copy-done.1 = f32[2,64,1024]{2,1,0:T(8,128)S(1)} copy-done((f32[2,64,1024]{2,1,0:T(8,128)S(1)}, f32[2,64,1024]{2,1,0:T(8,128)}, u32[]{:S(2)}) %copy-start.1) | copy-done | bytes 524312
  2.1 0.0 copy-start.2
  2.1 0.9 %copy-done.2 = f32[2,64,512]{2,1,0:T(8,128)S(1)} copy-done((f32[2,64,512]{2,1,0:T(8,128)S(1)}, f32[2,64,512]{2,1,0:T(8,128)}, u32[]{:S(2)}) %copy-start.2) | copy-done | bytes 262168
  3.0 82.0 %shard_map.37 = f32[1024,128]{1,0:T(8,128)S(1)} custom-call(f32[1024,128]{1,0:T(8,128)S(1)} %copy-done, f32[2,64,1024]{2,1,0:T(8,128)S(1)} %copy-done.1, f32[2,64,512]{2,1,0:T(8,128)S(1)} %copy-done.2), custom_call_target="tpu_custom_call" | custom-call | tf_op jit(solution)/shard_map/pallas_call | solution.py:226
  85.0 0.8 copy.5
Async XLA Ops:
  0.0 1.0 %copy-start = (f32[1024,128]{1,0:T(8,128)S(1)}, f32[1024,128]{1,0:T(8,128)}, u32[]{:S(2)}) copy-start(f32[1024,128]{1,0:T(8,128)} %b_hbm.1) | copy-start | bytes 1572868
  1.0 1.0 %copy-start.1 = (f32[2,64,1024]{2,1,0:T(8,128)S(1)}, f32[2,64,1024]{2,1,0:T(8,128)}, u32[]{:S(2)}) copy-start(f32[2,64,1024]{2,1,0:T(8,128)} %f_hbm.1) | copy-start | bytes 1572868
  2.1 0.9 %copy-start.2 = (f32[2,64,512]{2,1,0:T(8,128)S(1)}, f32[2,64,512]{2,1,0:T(8,128)}, u32[]{:S(2)}) copy-start(f32[2,64,512]{2,1,0:T(8,128)} %inv_hbm.1) | copy-start | bytes 786436

commit v2 on v1

--- a/solution.py
+++ b/solution.py
@@ -1,5 +1,3 @@
-import functools
-
 import jax
 import jax.numpy as jnp
 from jax import lax
@@ -11,15 +9,15 @@
 HIGHEST = lax.Precision.HIGHEST
 PLANE = 32
 CHUNK = 16
-HELPERS = ((1, 3, 4), (28, 5, 7))
-
-
-def kernel(b_hbm, f_hbm, inv_hbm, o_ref, bv, fall, invf, fb, xb, loc, ag_s, ag_r, in_s, in_r, fb_s, fb_r, sc_s, sc_r, ex_s, ex_r):
+
+
+def kernel(b_hbm, f_hbm, inv_hbm, o_ref, bv, fall, invf, fb, xb, loc, ag_s, ag_r, sb_s, sb_r, in_s, in_r, fb_s, fb_r, sc_s, sc_r, ex_s, ex_r, ready):
     r, c = lax.axis_index("rows"), lax.axis_index("cols")
     m, zh = r // 2, r % 2
     zl, core = c // 2, c % 2
     sib = zl * 2 + 1 - core
     root = r == 0
+    other = jnp.logical_not(root)
 
     def remote(src, dst, s, rs, row, col):
         return pltpu.make_async_remote_copy(
@@ -31,23 +29,16 @@
 
     def rows_of(col):
         return pl.ds(pl.multiple_of(col * 64, 64), 64)
+
+    duty = m - 1
+    duty_p, duty_d = duty // 12, duty % 3 + 1
+    helping = (zh == 0) & (m >= 1) & (m <= 24) & ((duty % 12) // 3 == zl)
 
     mine = rows_of(c)
     get_b = pltpu.make_async_copy(b_hbm, bv, loc.at[0])
     get_f = pltpu.make_async_copy(f_hbm, fall.at[:, mine], loc.at[1])
     get_fb = pltpu.make_async_copy(f_hbm.at[0, :, pl.ds(512, 512)], fb.at[mine], loc.at[1])
     get_inv = pltpu.make_async_copy(inv_hbm, invf.at[:, mine], loc.at[2])
-    get_b.start()
-
-    @pl.when(root)
-    def _():
-        get_fb.start()
-        get_inv.start()
-
-    @pl.when(jnp.logical_not(root))
-    def _():
-        get_f.start()
-
     barrier = pltpu.get_barrier_semaphore()
 
     def tell(row, col):
@@ -57,38 +48,43 @@
     for d in (1, 2, 3):
         tell(r, away(d))
 
-    def tell_plane(j, _):
-        tell(((m + j) % PLANE) * 2 + zh, c)
-        return 0
-
-    lax.fori_loop(1, PLANE, tell_plane, 0)
-
-    @pl.when(zh == 1)
-    def _():
-        tell(0, c)
-
     @pl.when(root)
     def _():
+        get_inv.start()
+        get_fb.start()
         for p in range(2):
             for d in (1, 2, 3):
-                tell(HELPERS[p][d - 1] * 2, ((zl + 4 - d) % 4) * 2 + core)
-        pl.semaphore_wait(barrier, 4 + 31 + 32)
-
-    helping = functools.reduce(jnp.logical_or, [r == h * 2 for line in HELPERS for h in line])
-
+                source = (zl + 4 - d) % 4
+                tell((p * 12 + source * 3 + d) * 2, source * 2 + core)
+
+        def tell_all(j, _):
+            tell(j, c)
+            return 0
+
+        lax.fori_loop(1, 2 * PLANE, tell_all, 0)
+        get_b.start()
+        pl.semaphore_wait(barrier, 4)
+
+    @pl.when(other)
+    def _():
+        get_f.start()
+        get_b.start()
+
+        def tell_plane(j, _):
+            peer = ((m + j) % PLANE) * 2 + zh
+
+            @pl.when(peer > 0)
+            def _():
+                tell(peer, c)
+            return 0
+
+        lax.fori_loop(1, PLANE, tell_plane, 0)
+        pl.semaphore_wait(barrier, 4 + 30 + zh + 1 + helping.astype(jnp.int32))
+
+    duty_copy = remote(inv_hbm.at[duty_p], invf.at[duty_p, mine], in_s.at[duty_p, duty_d], in_r.at[duty_p, duty_d], 0, away(duty_d))
     @pl.when(helping)
     def _():
-        pl.semaphore_wait(barrier, 4 + 31 + 1)
-
-    @pl.when(jnp.logical_not(jnp.logical_or(root, helping)))
-    def _():
-        pl.semaphore_wait(barrier, 4 + 31)
-
-    for p in range(2):
-        for d in (1, 2, 3):
-            @pl.when(r == HELPERS[p][d - 1] * 2)
-            def _():
-                remote(inv_hbm.at[p], invf.at[p, mine], in_s.at[p, d], in_r.at[p, d], 0, away(d)).start()
+        duty_copy.start()
 
     def chunk(x, i):
         return xb.at[x, pl.ds(pl.multiple_of(i * CHUNK, CHUNK), CHUNK)]
@@ -124,23 +120,24 @@
     @pl.when(root)
     def _():
         get_inv.wait()
-        get_fb.wait()
         own_inv = [remote(invf.at[p, mine], invf.at[p, mine], in_s.at[p, 0], in_r.at[p, 0], 0, sib) for p in range(2)]
         own_fb = [remote(fb.at[mine], fb.at[mine], fb_s.at[d], fb_r.at[d], 0, sib if d == 0 else away(d)) for d in range(4)]
-        for copy in own_inv + own_fb:
+        own_inv[0].start()
+        get_fb.wait()
+        for copy in own_fb + own_inv[1:]:
             copy.start()
         relays = []
 
-        def relay(ref_of, s, rs, arrive_s, arrive_r):
+        def relay(ref_of, s, rs):
             for d in (1, 2, 3):
                 got = ref_of(rows_of(away(4 - d)))
-                remote(got, got, arrive_s.at[d], arrive_r.at[d], 0, sib).wait_recv()
+                remote(got, got, s.at[d], rs.at[d], 0, sib).wait_recv()
                 on = remote(got, got, s.at[d + 3], rs.at[d + 3], 0, sib)
                 on.start()
                 relays.append(on)
 
         for p in range(2):
-            relay(lambda rows: invf.at[p, rows], in_s.at[p], in_r.at[p], in_s.at[p], in_r.at[p])
+            relay(lambda rows: invf.at[p, rows], in_s.at[p], in_r.at[p])
         own_inv[0].wait_recv()
         for copy in relays[:3]:
             copy.wait_recv()
@@ -148,9 +145,10 @@
         first = jnp.dot(invf[0], bv[0:512], precision=HIGHEST, preferred_element_type=jnp.float32)
         o_ref[0:512] = first
         xb[0] = blocks_across(first)
+        pl.semaphore_wait(ready, 63)
         scatter(0)
         exchange(0)
-        relay(lambda rows: fb.at[rows], fb_s, fb_r, fb_s, fb_r)
+        relay(lambda rows: fb.at[rows], fb_s, fb_r)
         own_fb[0].wait_recv()
         for copy in relays[6:]:
             copy.wait_recv()
@@ -171,27 +169,72 @@
             remote(first_rows(x, 32), first_rows(x, 32), sc_s.at[x, 1], sc_r.at[x], 1, c).wait_send()
             remote(first_rows(x, 31), first_rows(x, 31), ex_s.at[x], ex_r.at[x], 1, c).wait_send()
 
-    @pl.when(jnp.logical_not(root))
-    def _():
+    def has_source(way, step):
+        return zl >= step + 1 if way == 0 else zl <= 2 - step
+
+    def has_target(way):
+        return zl <= 2 if way == 0 else zl >= 1
+
+    def shard_at(way, step, p):
+        return fall.at[p, rows_of(away(3 - step if way == 0 else 1 + step))]
+
+    def along(way, step, p):
+        piece = fall.at[p, mine] if step == 0 else shard_at(way, step - 1, p)
+        return remote(piece, piece, ag_s.at[way, step, p], ag_r.at[way, step, p], r, away(1 if way == 0 else 3))
+
+    def arrived(way, step, p):
+        piece = shard_at(way, step, p)
+        return remote(piece, piece, ag_s.at[way, step, p], ag_r.at[way, step, p], r, sib)
+
+    def across(way, step, p):
+        piece = shard_at(way, step, p)
+        return remote(piece, piece, sb_s.at[1 + way * 3 + step, p], sb_r.at[1 + way * 3 + step, p], r, sib)
+
+    def own_across(p):
+        return remote(fall.at[p, mine], fall.at[p, mine], sb_s.at[0, p], sb_r.at[0, p], r, sib)
+
+    def take(step, p):
+        for way in range(2):
+            @pl.when(has_source(way, step))
+            def _():
+                arrived(way, step, p).wait_recv()
+                if step < 2:
+                    @pl.when(has_target(way))
+                    def _():
+                        along(way, step + 1, p).start()
+                across(way, step, p).start()
+
+    @pl.when(other)
+    def _():
+        pl.semaphore_signal(ready, inc=1, device_id={"rows": 0, "cols": c}, device_id_type=MESH)
         get_f.wait()
-        own = [remote(fall.at[:, mine], fall.at[:, mine], ag_s.at[d], ag_r.at[d], r, sib if d == 0 else away(d)) for d in range(4)]
-        for copy in own:
-            copy.start()
-        for x in range(2):
+        for p in range(2):
+            for way in range(2):
+                @pl.when(has_target(way))
+                def _():
+                    along(way, 0, p).start()
+        for p in range(2):
+            own_across(p).start()
+        take(0, 0)
+        take(0, 1)
+
+        def solved(x):
             remote(chunk(x, m), chunk(x, m), sc_s.at[x, 0], sc_r.at[x], 0, c).wait_recv()
             exchange(x)
-        relays = []
-        for d in (1, 2, 3):
-            own[d].wait_recv()
-            got = fall.at[:, rows_of(away(4 - d))]
-            on = remote(got, got, ag_s.at[d + 3], ag_r.at[d + 3], r, sib)
-            on.start()
-            relays.append(on)
-        own[0].wait_recv()
-        for copy in relays:
-            copy.wait_recv()
+
+        solved(0)
+        take(1, 0)
+        take(1, 1)
+        solved(1)
         get_b.wait()
         for x in range(2):
+            take(2, x)
+            own_across(x).wait_recv()
+            for step in range(3):
+                for way in range(2):
+                    @pl.when(has_source(way, step))
+                    def _():
+                        across(way, step, x).wait_recv()
             remote(first_rows(x, 31), first_rows(x, 31), ex_s.at[x], ex_r.at[x], 0, c).wait_recv()
             left = jnp.concatenate([xb[x, i * 128:(i + 1) * 128] for i in range(4)], axis=1)
             src = bv if x == 0 else o_ref
@@ -203,13 +246,21 @@
                 return 0
 
             lax.fori_loop(0, 4, update, 0)
-        for copy in own + relays:
-            copy.wait_send()
-        for p in range(2):
-            for d in (1, 2, 3):
-                @pl.when(r == HELPERS[p][d - 1] * 2)
-                def _():
-                    remote(inv_hbm.at[p], invf.at[p, mine], in_s.at[p, d], in_r.at[p, d], 0, away(d)).wait_send()
+        for p in range(2):
+            own_across(p).wait_send()
+            for way in range(2):
+                for step in range(3):
+                    @pl.when(has_source(way, step))
+                    def _():
+                        across(way, step, p).wait_send()
+                    sent = has_target(way) if step == 0 else has_target(way) & has_source(way, step - 1)
+
+                    @pl.when(sent)
+                    def _():
+                        along(way, step, p).wait_send()
+        @pl.when(helping)
+        def _():
+            duty_copy.wait_send()
         for x in range(2):
             @pl.when(zh == 0)
             def _():
@@ -235,14 +286,16 @@
             pltpu.VMEM((512, 512), jnp.float32),
             pltpu.VMEM((2, 512, 128), jnp.float32),
             dma((3,)),
-            dma((7,)), dma((7,)),
+            dma((2, 3, 2)), dma((2, 3, 2)),
+            dma((7, 2)), dma((7, 2)),
             dma((2, 7)), dma((2, 7)),
             dma((7,)), dma((7,)),
             dma((2, 2)), dma((2,)),
             dma((2,)), dma((2,)),
+            pltpu.SemaphoreType.REGULAR,
         ],
         compiler_params=pltpu.CompilerParams(
-            collective_id=0, has_side_effects=True, vmem_limit_bytes=48 << 20),
+            collective_id=0, has_side_effects=True, vmem_limit_bytes=60 << 20),
     )(cross_kernel, factor_panels, block_inverses)
 
 

time: 86.2 us -> 62.9 us (0.73)
  the two profiles are of different devices: /device:TPU:2 before, /device:TPU:5 now
where the time goes in v2:
time: 62.9 us; the launch traced here: 62.8 us
  Pallas kernels  60.9 us (97%)
  local copies, waits for them, and re-layouts  1.87 us (3%)
    pallas_call x1, Pallas kernels, on_device(): pl.pallas_call(kernel, out_shape=jax.ShapeDtypeStruct(cross_kernel.shape,...  60.9 us
    unnamed x1, local copies, waits for them, and re-layouts  1.87 us

profile of v2, /device:TPU:5, one launch (start us, length us, event | category | flops | bytes accessed | tf_op | source)
XLA Modules:
  0.0 62.8 jit_solution(586005179506844717)
XLA Ops:
  0.0 60.9 %shard_map.37 = f32[1024,128]{1,0:T(8,128)} custom-call(f32[1024,128]{1,0:T(8,128)} %b_hbm.1, f32[2,64,1024]{2,1,0:T(8,128)} %f_hbm.1, f32[2,64,512]{2,1,0:T(8,128)} %inv_hbm.1), custom_call_target="tpu_custom_call" | custom-call | tf_op jit(solution)/shard_map/pallas_call | solution.py:277
  60.9 1.9 %copy.5 = f32[1024,128]{1,0:T(8,128)} copy(f32[1024,128]{1,0:T(8,128)} %shard_map.37) | data formatting | bytes 1048576

commit v3 on v2

--- a/solution.py
+++ b/solution.py
@@ -6,12 +6,32 @@
 from jax.sharding import PartitionSpec as P
 
 MESH = pl.DeviceIdType.MESH
-HIGHEST = lax.Precision.HIGHEST
 PLANE = 32
 CHUNK = 16
-
-
-def kernel(b_hbm, f_hbm, inv_hbm, o_ref, bv, fall, invf, fb, xb, loc, ag_s, ag_r, sb_s, sb_r, in_s, in_r, fb_s, fb_r, sc_s, sc_r, ex_s, ex_r, ready):
+FLOWS = tuple(
+    (p, source, target, 2 * lines[p] + (abs(source - target) == 3))
+    for source, target, lines in (
+        (1, 0, (2, 2)), (2, 0, (3, 1)), (3, 0, (1, 3)),
+        (0, 1, (1, 2)), (2, 1, (2, 3)), (3, 1, (3, 1)),
+        (0, 2, (3, 2)), (1, 2, (1, 3)), (3, 2, (2, 1)),
+        (0, 3, (1, 3)), (1, 3, (2, 2)), (2, 3, (3, 1)),
+    )
+    for p in range(2)
+)
+
+
+def halves(value):
+    high = value.astype(jnp.bfloat16)
+    return high, (value - high.astype(jnp.float32)).astype(jnp.bfloat16)
+
+
+def product(left, right):
+    (a, b), (c, d) = halves(left), halves(right)
+    dot = lambda x, y: jnp.dot(x, y, preferred_element_type=jnp.float32)
+    return dot(a, c) + (dot(a, d) + dot(b, c))
+
+
+def kernel(b_hbm, f_hbm, inv_hbm, o_ref, bv, fall, invf, fb, xb, total, loc, ag_s, ag_r, sb_s, sb_r, in_s, in_r, on_s, on_r, fb_s, fb_r, sc_s, sc_r, ex_s, ex_r, ready):
     r, c = lax.axis_index("rows"), lax.axis_index("cols")
     m, zh = r // 2, r % 2
     zl, core = c // 2, c % 2
@@ -30,10 +50,6 @@
     def rows_of(col):
         return pl.ds(pl.multiple_of(col * 64, 64), 64)
 
-    duty = m - 1
-    duty_p, duty_d = duty // 12, duty % 3 + 1
-    helping = (zh == 0) & (m >= 1) & (m <= 24) & ((duty % 12) // 3 == zl)
-
     mine = rows_of(c)
     get_b = pltpu.make_async_copy(b_hbm, bv, loc.at[0])
     get_f = pltpu.make_async_copy(f_hbm, fall.at[:, mine], loc.at[1])
@@ -44,21 +60,21 @@
     def tell(row, col):
         pl.semaphore_signal(barrier, inc=1, device_id={"rows": row, "cols": col}, device_id_type=MESH)
 
-    tell(r, sib)
     for d in (1, 2, 3):
         tell(r, away(d))
+    tell(r, sib)
 
     @pl.when(root)
     def _():
+        get_fb.start()
         get_inv.start()
-        get_fb.start()
-        for p in range(2):
-            for d in (1, 2, 3):
-                source = (zl + 4 - d) % 4
-                tell((p * 12 + source * 3 + d) * 2, source * 2 + core)
+        for p, source, target, row in FLOWS:
+            @pl.when(zl == target)
+            def _():
+                tell(row, source * 2 + core)
 
         def tell_all(j, _):
-            tell(j, c)
+            tell(2 * PLANE - j, c)
             return 0
 
         lax.fori_loop(1, 2 * PLANE, tell_all, 0)
@@ -69,22 +85,22 @@
     def _():
         get_f.start()
         get_b.start()
-
-        def tell_plane(j, _):
-            peer = ((m + j) % PLANE) * 2 + zh
-
-            @pl.when(peer > 0)
-            def _():
-                tell(peer, c)
-            return 0
-
-        lax.fori_loop(1, PLANE, tell_plane, 0)
-        pl.semaphore_wait(barrier, 4 + 30 + zh + 1 + helping.astype(jnp.int32))
-
-    duty_copy = remote(inv_hbm.at[duty_p], invf.at[duty_p, mine], in_s.at[duty_p, duty_d], in_r.at[duty_p, duty_d], 0, away(duty_d))
-    @pl.when(helping)
-    def _():
-        duty_copy.start()
+        duties = sum(((r == row) & (zl == source)).astype(jnp.int32) for p, source, target, row in FLOWS)
+        pl.semaphore_wait(barrier, 4 + 1 + duties)
+        pl.semaphore_signal(ready, inc=1, device_id={"rows": 0, "cols": c}, device_id_type=MESH)
+
+    def inverse_rows(p, source, core_of):
+        return (p, pl.ds(pl.multiple_of(source * 128 + core_of * 64, 64), 64), pl.ds(0, (source + 1) * 128))
+
+    def duty(p, source, target):
+        return remote(
+            inv_hbm.at[p, :, pl.ds(0, (source + 1) * 128)], invf.at[inverse_rows(p, source, core)],
+            in_s.at[p, target], in_r.at[p, source], 0, target * 2 + core)
+
+    for p, source, target, row in FLOWS:
+        @pl.when((r == row) & (zl == source))
+        def _():
+            duty(p, source, target).start()
 
     def chunk(x, i):
         return xb.at[x, pl.ds(pl.multiple_of(i * CHUNK, CHUNK), CHUNK)]
@@ -114,56 +130,66 @@
     def first_rows(x, n):
         return xb.at[x, pl.ds(0, n * CHUNK)]
 
-    def blocks_across(value):
-        return jnp.concatenate([value[i * 128:(i + 1) * 128].T for i in range(4)], axis=0)
-
     @pl.when(root)
     def _():
+        get_fb.wait()
+        own_fb = [remote(fb.at[mine], fb.at[mine], fb_s.at[d], fb_r.at[d], 0, sib if d == 0 else away(d)) for d in range(4)]
+        for copy in own_fb[1:] + own_fb[:1]:
+            copy.start()
         get_inv.wait()
-        own_inv = [remote(invf.at[p, mine], invf.at[p, mine], in_s.at[p, 0], in_r.at[p, 0], 0, sib) for p in range(2)]
-        own_fb = [remote(fb.at[mine], fb.at[mine], fb_s.at[d], fb_r.at[d], 0, sib if d == 0 else away(d)) for d in range(4)]
-        own_inv[0].start()
-        get_fb.wait()
-        for copy in own_fb + own_inv[1:]:
-            copy.start()
-        relays = []
-
-        def relay(ref_of, s, rs):
-            for d in (1, 2, 3):
-                got = ref_of(rows_of(away(4 - d)))
-                remote(got, got, s.at[d], rs.at[d], 0, sib).wait_recv()
-                on = remote(got, got, s.at[d + 3], rs.at[d + 3], 0, sib)
-                on.start()
-                relays.append(on)
-
-        for p in range(2):
-            relay(lambda rows: invf.at[p, rows], in_s.at[p], in_r.at[p])
-        own_inv[0].wait_recv()
-        for copy in relays[:3]:
-            copy.wait_recv()
+
+        def inverse_on(p, source, core_of):
+            piece = invf.at[inverse_rows(p, source, core_of)]
+            return remote(piece, piece, on_s.at[p, source], on_r.at[p, source], 0, sib)
+
+        def inverse_arrived(p, source):
+            @pl.when(zl != source)
+            def _():
+                piece = invf.at[inverse_rows(p, source, core)]
+                remote(piece, piece, in_s.at[p, 0], in_r.at[p, source], 0, sib).wait_recv()
+            inverse_on(p, source, core).start()
+
+        def inverse_times(p, source, right):
+            inverse_on(p, source, 1 - core).wait_recv()
+            return product(invf[p, source * 128:(source + 1) * 128, 0:(source + 1) * 128], right)
+
+        for i in range(4):
+            inverse_arrived(0, i)
         get_b.wait()
-        first = jnp.dot(invf[0], bv[0:512], precision=HIGHEST, preferred_element_type=jnp.float32)
-        o_ref[0:512] = first
-        xb[0] = blocks_across(first)
+        for i in range(4):
+            block = inverse_times(0, i, bv[0:(i + 1) * 128])
+            o_ref[i * 128:(i + 1) * 128] = block
+            xb[0, i * 128:(i + 1) * 128] = block.T
         pl.semaphore_wait(ready, 63)
         scatter(0)
-        exchange(0)
-        relay(lambda rows: fb.at[rows], fb_s, fb_r)
+        fb_on = []
+        for d in (1, 2, 3):
+            got = fb.at[rows_of(away(4 - d))]
+            remote(got, got, fb_s.at[d], fb_r.at[d], 0, sib).wait_recv()
+            on = remote(got, got, fb_s.at[d + 3], fb_r.at[d + 3], 0, sib)
+            on.start()
+            fb_on.append(on)
+        for i in range(4):
+            inverse_arrived(1, i)
         own_fb[0].wait_recv()
-        for copy in relays[6:]:
+        for copy in fb_on:
             copy.wait_recv()
-        rest = bv[512:1024] - lax.dot_general(
-            fb[...], o_ref[0:512], (((0,), (0,)), ((), ())), precision=HIGHEST, preferred_element_type=jnp.float32)
-        own_inv[1].wait_recv()
-        for copy in relays[3:6]:
-            copy.wait_recv()
-        second = jnp.dot(invf[1], rest, precision=HIGHEST, preferred_element_type=jnp.float32)
-        o_ref[512:1024] = second
-        xb[1] = blocks_across(second)
+        for i in range(4):
+            cut = slice(i * 128, (i + 1) * 128)
+            took = product(fb[:, cut].T, o_ref[0:512])
+            bv[512 + i * 128:512 + (i + 1) * 128] = bv[512 + i * 128:512 + (i + 1) * 128] - took
+        for i in range(4):
+            block = inverse_times(1, i, bv[512:512 + (i + 1) * 128])
+            o_ref[512 + i * 128:512 + (i + 1) * 128] = block
+            xb[1, i * 128:(i + 1) * 128] = block.T
         scatter(1)
         exchange(1)
-        for copy in own_inv + own_fb + relays:
+        exchange(0)
+        for copy in own_fb + fb_on:
             copy.wait_send()
+        for p in range(2):
+            for i in range(4):
+                inverse_on(p, i, core).wait_send()
         for x in range(2):
             remote(first_rows(x, 31), first_rows(x, 31), sc_s.at[x, 0], sc_r.at[x], 1, c).wait_send()
             remote(first_rows(x, 32), first_rows(x, 32), sc_s.at[x, 1], sc_r.at[x], 1, c).wait_send()
@@ -206,7 +232,6 @@
 
     @pl.when(other)
     def _():
-        pl.semaphore_signal(ready, inc=1, device_id={"rows": 0, "cols": c}, device_id_type=MESH)
         get_f.wait()
         for p in range(2):
             for way in range(2):
@@ -237,12 +262,14 @@
                         across(way, step, x).wait_recv()
             remote(first_rows(x, 31), first_rows(x, 31), ex_s.at[x], ex_r.at[x], 0, c).wait_recv()
             left = jnp.concatenate([xb[x, i * 128:(i + 1) * 128] for i in range(4)], axis=1)
-            src = bv if x == 0 else o_ref
 
             def update(i, _):
                 cut = pl.ds(pl.multiple_of(i * 256, 256), 256)
-                took = jnp.dot(left, fall[x, :, cut], precision=HIGHEST, preferred_element_type=jnp.float32)
-                o_ref[cut] = src[cut] - took.T
+                took = product(left, fall[x, :, cut])
+                if x == 0:
+                    total[:, cut] = took
+                else:
+                    o_ref[cut] = bv[cut] - (total[:, cut] + took).T
                 return 0
 
             lax.fori_loop(0, 4, update, 0)
@@ -258,9 +285,10 @@
                     @pl.when(sent)
                     def _():
                         along(way, step, p).wait_send()
-        @pl.when(helping)
-        def _():
-            duty_copy.wait_send()
+        for p, source, target, row in FLOWS:
+            @pl.when((r == row) & (zl == source))
+            def _():
+                duty(p, source, target).wait_send()
         for x in range(2):
             @pl.when(zh == 0)
             def _():
@@ -285,18 +313,20 @@
             pltpu.VMEM((2, 512, 512), jnp.float32),
             pltpu.VMEM((512, 512), jnp.float32),
             pltpu.VMEM((2, 512, 128), jnp.float32),
+            pltpu.VMEM((128, 1024), jnp.float32),
             dma((3,)),
             dma((2, 3, 2)), dma((2, 3, 2)),
             dma((7, 2)), dma((7, 2)),
-            dma((2, 7)), dma((2, 7)),
+            dma((2, 4)), dma((2, 4)),
+            dma((2, 4)), dma((2, 4)),
             dma((7,)), dma((7,)),
             dma((2, 2)), dma((2,)),
             dma((2,)), dma((2,)),
             pltpu.SemaphoreType.REGULAR,
         ],
         compiler_params=pltpu.CompilerParams(
-            collective_id=0, has_side_effects=True, vmem_limit_bytes=60 << 20),
-    )(cross_kernel, factor_panels, block_inverses)
+            collective_id=0, has_side_effects=True, vmem_limit_bytes=48 << 20),
+    )(*[pltpu.with_memory_space_constraint(x, pltpu.HBM) for x in (cross_kernel, factor_panels, block_inverses)])
 
 
 def solution(mesh):

time: 62.9 us -> 50.6 us (0.80)
  the two profiles are of different devices: /device:TPU:5 before, /device:TPU:2 now
where the time goes in v3:
time: 50.6 us; the launch traced here: 50.5 us
  Pallas kernels  49.7 us (98%)
  local copies, waits for them, and re-layouts  0.8 us (2%)
    pallas_call x1, Pallas kernels, on_device(): pl.pallas_call(kernel, out_shape=jax.ShapeDtypeStruct(cross_kernel.shape,...  49.7 us

profile of v3, /device:TPU:2, one launch (start us, length us, event | category | flops | bytes accessed | tf_op | source)
XLA Modules:
  0.0 50.5 jit_solution(17771382052050133948)
XLA Ops:
  0.0 49.7 %shard_map.37 = f32[1024,128]{1,0:T(8,128)S(1)} custom-call(f32[1024,128]{1,0:T(8,128)} %b_hbm.1, f32[2,64,1024]{2,1,0:T(8,128)} %f_hbm.1, f32[2,64,512]{2,1,0:T(8,128)} %inv_hbm.1), custom_call_target="tpu_custom_call" | custom-call | tf_op jit(solution)/shard_map/pallas_call | solution.py:305
  49.7 0.8 %copy.5 = f32[1024,128]{1,0:T(8,128)} copy(f32[1024,128]{1,0:T(8,128)S(1)} %shard_map.37) | data formatting | bytes 1048576

commit v4 on v3

--- a/solution.py
+++ b/solution.py
@@ -8,13 +8,14 @@
 MESH = pl.DeviceIdType.MESH
 PLANE = 32
 CHUNK = 16
+STRIDE = 13
 FLOWS = tuple(
-    (p, source, target, 2 * lines[p] + (abs(source - target) == 3))
+    (p, source, target, lines[p])
     for source, target, lines in (
-        (1, 0, (2, 2)), (2, 0, (3, 1)), (3, 0, (1, 3)),
-        (0, 1, (1, 2)), (2, 1, (2, 3)), (3, 1, (3, 1)),
-        (0, 2, (3, 2)), (1, 2, (1, 3)), (3, 2, (2, 1)),
-        (0, 3, (1, 3)), (1, 3, (2, 2)), (2, 3, (3, 1)),
+        (1, 0, (0, 4)), (2, 0, (0, 3)), (3, 0, (3, 7)),
+        (0, 1, (4, 2)), (2, 1, (2, 6)), (3, 1, (5, 7)),
+        (0, 2, (7, 5)), (1, 2, (6, 4)), (3, 2, (2, 4)),
+        (0, 3, (3, 5)), (1, 3, (0, 7)), (2, 3, (0, 2)),
     )
     for p in range(2)
 )
@@ -31,7 +32,7 @@
     return dot(a, c) + (dot(a, d) + dot(b, c))
 
 
-def kernel(b_hbm, f_hbm, inv_hbm, o_ref, bv, fall, invf, fb, xb, total, loc, ag_s, ag_r, sb_s, sb_r, in_s, in_r, on_s, on_r, fb_s, fb_r, sc_s, sc_r, ex_s, ex_r, ready):
+def kernel(b_hbm, f_hbm, inv_hbm, o_ref, bv, fall, invf, fb, xb, total, loc, ag_s, ag_r, sb_s, sb_r, in_s, in_r, on_s, on_r, fb_s, fb_r, sc_s, sc_r, ex_s, ex_r, ready, above):
     r, c = lax.axis_index("rows"), lax.axis_index("cols")
     m, zh = r // 2, r % 2
     zl, core = c // 2, c % 2
@@ -60,18 +61,27 @@
     def tell(row, col):
         pl.semaphore_signal(barrier, inc=1, device_id={"rows": row, "cols": col}, device_id_type=MESH)
 
-    for d in (1, 2, 3):
-        tell(r, away(d))
     tell(r, sib)
+
+    def open_down(reach):
+        for d in range(1, reach + 1):
+            @pl.when(zl >= d)
+            def _():
+                pl.semaphore_signal(above, inc=1, device_id={"rows": r, "cols": c - 2 * d}, device_id_type=MESH)
 
     @pl.when(root)
     def _():
+        for d in range(1, 4):
+            @pl.when(zl + d <= 3)
+            def _():
+                tell(r, c + 2 * d)
         get_fb.start()
         get_inv.start()
         for p, source, target, row in FLOWS:
-            @pl.when(zl == target)
-            def _():
-                tell(row, source * 2 + core)
+            if row > 0:
+                @pl.when(zl == target)
+                def _():
+                    tell(row, source * 2 + core)
 
         def tell_all(j, _):
             tell(2 * PLANE - j, c)
@@ -79,14 +89,19 @@
 
         lax.fori_loop(1, 2 * PLANE, tell_all, 0)
         get_b.start()
-        pl.semaphore_wait(barrier, 4)
+        pl.semaphore_wait(barrier, zl + 1)
+        open_down(3)
 
     @pl.when(other)
     def _():
+        @pl.when(zl < 3)
+        def _():
+            tell(r, c + 2)
         get_f.start()
         get_b.start()
-        duties = sum(((r == row) & (zl == source)).astype(jnp.int32) for p, source, target, row in FLOWS)
-        pl.semaphore_wait(barrier, 4 + 1 + duties)
+        duties = sum(((r == row) & (zl == source)).astype(jnp.int32) for p, source, target, row in FLOWS if row > 0)
+        pl.semaphore_wait(barrier, jnp.minimum(zl, 1) + 1 + 1 + duties)
+        open_down(1)
         pl.semaphore_signal(ready, inc=1, device_id={"rows": 0, "cols": c}, device_id_type=MESH)
 
     def inverse_rows(p, source, core_of):
@@ -98,27 +113,31 @@
             in_s.at[p, target], in_r.at[p, source], 0, target * 2 + core)
 
     for p, source, target, row in FLOWS:
-        @pl.when((r == row) & (zl == source))
-        def _():
-            duty(p, source, target).start()
+        if row > 0:
+            @pl.when((r == row) & (zl == source))
+            def _():
+                duty(p, source, target).start()
 
     def chunk(x, i):
         return xb.at[x, pl.ds(pl.multiple_of(i * CHUNK, CHUNK), CHUNK)]
 
     def scatter(x):
-        def to_one(i, _):
-            remote(chunk(x, i), chunk(x, i), sc_s.at[x, 1], sc_r.at[x], i * 2 + 1, c).start()
-
-            @pl.when(i > 0)
-            def _():
-                remote(chunk(x, i), chunk(x, i), sc_s.at[x, 0], sc_r.at[x], i * 2, c).start()
+        def to_near(i, _):
+            to = i * STRIDE % PLANE
+            remote(chunk(x, to), chunk(x, to), sc_s.at[x, 0], sc_r.at[x], to * 2, c).start()
             return 0
 
-        lax.fori_loop(0, PLANE, to_one, 0)
+        def to_far(i, _):
+            to = i * STRIDE % PLANE
+            remote(chunk(x, to), chunk(x, to), sc_s.at[x, 1], sc_r.at[x], to * 2 + 1, c).start()
+            return 0
+
+        lax.fori_loop(1, PLANE, to_near, 0)
+        lax.fori_loop(0, PLANE, to_far, 0)
 
     def exchange(x):
         def to_one(j, _):
-            peer = ((m + j) % PLANE) * 2 + zh
+            peer = ((m + j * STRIDE) % PLANE) * 2 + zh
 
             @pl.when(peer > 0)
             def _():
@@ -132,10 +151,30 @@
 
     @pl.when(root)
     def _():
+        def own_fb(target):
+            return remote(fb.at[mine], fb.at[mine], fb_s.at[target], fb_r.at[zl], 0, target * 2 + core)
+
+        own_fb_across = remote(fb.at[mine], fb.at[mine], fb_s.at[4], fb_r.at[4], 0, sib)
+
+        def along_line(up):
+            for p, source, target, row in FLOWS:
+                if row == 0 and (target > source) == up:
+                    @pl.when(zl == source)
+                    def _():
+                        duty(p, source, target).start()
+            for target in (3, 2, 1, 0):
+                @pl.when(zl < target if up else zl > target)
+                def _():
+                    own_fb(target).start()
+
         get_fb.wait()
-        own_fb = [remote(fb.at[mine], fb.at[mine], fb_s.at[d], fb_r.at[d], 0, sib if d == 0 else away(d)) for d in range(4)]
-        for copy in own_fb[1:] + own_fb[:1]:
-            copy.start()
+        along_line(False)
+
+        @pl.when(zl < 3)
+        def _():
+            pl.semaphore_wait(above, 3 - zl)
+        along_line(True)
+        own_fb_across.start()
         get_inv.wait()
 
         def inverse_on(p, source, core_of):
@@ -164,20 +203,18 @@
         scatter(0)
         fb_on = []
         for d in (1, 2, 3):
-            got = fb.at[rows_of(away(4 - d))]
-            remote(got, got, fb_s.at[d], fb_r.at[d], 0, sib).wait_recv()
-            on = remote(got, got, fb_s.at[d + 3], fb_r.at[d + 3], 0, sib)
+            source = (zl + d) % 4
+            got = fb.at[rows_of(source * 2 + core)]
+            remote(got, got, fb_s.at[0], fb_r.at[source], 0, sib).wait_recv()
+            on = remote(got, got, fb_s.at[4 + d], fb_r.at[4 + d], 0, sib)
             on.start()
             fb_on.append(on)
         for i in range(4):
             inverse_arrived(1, i)
-        own_fb[0].wait_recv()
-        for copy in fb_on:
-            copy.wait_recv()
-        for i in range(4):
-            cut = slice(i * 128, (i + 1) * 128)
-            took = product(fb[:, cut].T, o_ref[0:512])
-            bv[512 + i * 128:512 + (i + 1) * 128] = bv[512 + i * 128:512 + (i + 1) * 128] - took
+        for d in range(4):
+            (own_fb_across if d == 0 else fb_on[d - 1]).wait_recv()
+            shard = pl.ds(pl.multiple_of((zl + d) % 4 * 128, 128), 128)
+            bv[512:1024] = bv[512:1024] - product(fb[shard].T, o_ref[shard])
         for i in range(4):
             block = inverse_times(1, i, bv[512:512 + (i + 1) * 128])
             o_ref[512 + i * 128:512 + (i + 1) * 128] = block
@@ -185,15 +222,24 @@
         scatter(1)
         exchange(1)
         exchange(0)
-        for copy in own_fb + fb_on:
+        for copy in [own_fb_across] + fb_on:
             copy.wait_send()
+        for target in range(4):
+            @pl.when(zl != target)
+            def _():
+                own_fb(target).wait_send()
+        for p, source, target, row in FLOWS:
+            if row == 0:
+                @pl.when(zl == source)
+                def _():
+                    duty(p, source, target).wait_send()
         for p in range(2):
             for i in range(4):
                 inverse_on(p, i, core).wait_send()
         for x in range(2):
-            remote(first_rows(x, 31), first_rows(x, 31), sc_s.at[x, 0], sc_r.at[x], 1, c).wait_send()
-            remote(first_rows(x, 32), first_rows(x, 32), sc_s.at[x, 1], sc_r.at[x], 1, c).wait_send()
-            remote(first_rows(x, 31), first_rows(x, 31), ex_s.at[x], ex_r.at[x], 1, c).wait_send()
+            for sem in (sc_s.at[x, 0], ex_s.at[x]):
+                remote(first_rows(x, 31), first_rows(x, 31), sem, sc_r.at[x], 1, c).wait_send()
+            remote(xb.at[x], xb.at[x], sc_s.at[x, 1], sc_r.at[x], 1, c).wait_send()
 
     def has_source(way, step):
         return zl >= step + 1 if way == 0 else zl <= 2 - step
@@ -234,10 +280,15 @@
     def _():
         get_f.wait()
         for p in range(2):
-            for way in range(2):
-                @pl.when(has_target(way))
-                def _():
-                    along(way, 0, p).start()
+            @pl.when(has_target(1))
+            def _():
+                along(1, 0, p).start()
+
+        @pl.when(has_target(0))
+        def _():
+            pl.semaphore_wait(above, 1)
+            for p in range(2):
+                along(0, 0, p).start()
         for p in range(2):
             own_across(p).start()
         take(0, 0)
@@ -260,7 +311,7 @@
                     @pl.when(has_source(way, step))
                     def _():
                         across(way, step, x).wait_recv()
-            remote(first_rows(x, 31), first_rows(x, 31), ex_s.at[x], ex_r.at[x], 0, c).wait_recv()
+            remote(first_rows(x, 31), first_rows(x, 31), ex_s.at[x], ex_r.at[x], 1, c).wait_recv()
             left = jnp.concatenate([xb[x, i * 128:(i + 1) * 128] for i in range(4)], axis=1)
 
             def update(i, _):
@@ -286,9 +337,10 @@
                     def _():
                         along(way, step, p).wait_send()
         for p, source, target, row in FLOWS:
-            @pl.when((r == row) & (zl == source))
-            def _():
-                duty(p, source, target).wait_send()
+            if row > 0:
+                @pl.when((r == row) & (zl == source))
+                def _():
+                    duty(p, source, target).wait_send()
         for x in range(2):
             @pl.when(zh == 0)
             def _():
@@ -319,9 +371,10 @@
             dma((7, 2)), dma((7, 2)),
             dma((2, 4)), dma((2, 4)),
             dma((2, 4)), dma((2, 4)),
-            dma((7,)), dma((7,)),
+            dma((8,)), dma((8,)),
             dma((2, 2)), dma((2,)),
             dma((2,)), dma((2,)),
+            pltpu.SemaphoreType.REGULAR,
             pltpu.SemaphoreType.REGULAR,
         ],
         compiler_params=pltpu.CompilerParams(

time: 50.6 us -> 49.6 us (0.980)
  the two profiles are of different devices: /device:TPU:2 before, /device:TPU:13 now
where the time goes in v4:
time: 49.6 us; the launch traced here: 49.5 us
  Pallas kernels  48.7 us (98%)
  local copies, waits for them, and re-layouts  0.8 us (2%)
    pallas_call x1, Pallas kernels, on_device(): pl.pallas_call(kernel, out_shape=jax.ShapeDtypeStruct(cross_kernel.shape,...  48.7 us

profile of v4, /device:TPU:13, one launch (start us, length us, event | category | flops | bytes accessed | tf_op | source)
XLA Modules:
  0.0 49.5 jit_solution(3639077134373509967)
XLA Ops:
  0.0 48.7 %shard_map.37 = f32[1024,128]{1,0:T(8,128)S(1)} custom-call(f32[1024,128]{1,0:T(8,128)} %b_hbm.1, f32[2,64,1024]{2,1,0:T(8,128)} %f_hbm.1, f32[2,64,512]{2,1,0:T(8,128)} %inv_hbm.1), custom_call_target="tpu_custom_call" | custom-call | tf_op jit(solution)/shard_map/pallas_call | solution.py:357
  48.7 0.8 %copy.5 = f32[1024,128]{1,0:T(8,128)} copy(f32[1024,128]{1,0:T(8,128)S(1)} %shard_map.37) | data formatting | bytes 1048576

commit v5 on v4

--- a/solution.py
+++ b/solution.py
@@ -12,10 +12,10 @@
 FLOWS = tuple(
     (p, source, target, lines[p])
     for source, target, lines in (
-        (1, 0, (0, 4)), (2, 0, (0, 3)), (3, 0, (3, 7)),
+        (1, 0, (0, 4)), (2, 0, (6, 3)), (3, 0, (3, 7)),
         (0, 1, (4, 2)), (2, 1, (2, 6)), (3, 1, (5, 7)),
         (0, 2, (7, 5)), (1, 2, (6, 4)), (3, 2, (2, 4)),
-        (0, 3, (3, 5)), (1, 3, (0, 7)), (2, 3, (0, 2)),
+        (0, 3, (3, 5)), (1, 3, (6, 7)), (2, 3, (0, 2)),
     )
     for p in range(2)
 )

time: 49.6 us -> 48.9 us (0.986)
  Pallas kernels: 48.7 us -> 47.9 us
    pallas_call x1, Pallas kernels: 48.7 us -> 47.9 us  [on_device(): pl.pallas_call(kernel, out_shape=jax.ShapeDtypeStruct(cross_kernel.shape,...]
where the time goes in v5:
time: 48.9 us; the launch traced here: 48.7 us
  Pallas kernels  47.9 us (98%)
  local copies, waits for them, and re-layouts  0.8 us (2%)
    pallas_call x1, Pallas kernels, on_device(): pl.pallas_call(kernel, out_shape=jax.ShapeDtypeStruct(cross_kernel.shape,...  47.9 us

profile of v5, /device:TPU:13, one launch (start us, length us, event | category | flops | bytes accessed | tf_op | source)
XLA Modules:
  0.0 48.7 jit_solution(4621432398060374484)
XLA Ops:
  0.0 47.9 %shard_map.37 = f32[1024,128]{1,0:T(8,128)S(1)} custom-call(f32[1024,128]{1,0:T(8,128)} %b_hbm.1, f32[2,64,1024]{2,1,0:T(8,128)} %f_hbm.1, f32[2,64,512]{2,1,0:T(8,128)} %inv_hbm.1), custom_call_target="tpu_custom_call" | custom-call | tf_op jit(solution)/shard_map/pallas_call | solution.py:357
  48.0 0.8 %copy.5 = f32[1024,128]{1,0:T(8,128)} copy(f32[1024,128]{1,0:T(8,128)S(1)} %shard_map.37) | data formatting | bytes 1048576

commit v6 on v5

--- a/solution.py
+++ b/solution.py
@@ -8,14 +8,14 @@
 MESH = pl.DeviceIdType.MESH
 PLANE = 32
 CHUNK = 16
-STRIDE = 13
+STRIDE = 21
 FLOWS = tuple(
     (p, source, target, lines[p])
     for source, target, lines in (
-        (1, 0, (0, 4)), (2, 0, (6, 3)), (3, 0, (3, 7)),
+        (1, 0, (2, 4)), (2, 0, (6, 3)), (3, 0, (3, 7)),
         (0, 1, (4, 2)), (2, 1, (2, 6)), (3, 1, (5, 7)),
         (0, 2, (7, 5)), (1, 2, (6, 4)), (3, 2, (2, 4)),
-        (0, 3, (3, 5)), (1, 3, (6, 7)), (2, 3, (0, 2)),
+        (0, 3, (3, 5)), (1, 3, (6, 7)), (2, 3, (4, 2)),
     )
     for p in range(2)
 )

time: 48.9 us -> 48.8 us (level)
  the two profiles are of different devices: /device:TPU:13 before, /device:TPU:23 now
where the time goes in v6:
time: 48.8 us; the launch traced here: 48.7 us
  Pallas kernels  47.9 us (98%)
  local copies, waits for them, and re-layouts  0.8 us (2%)
    pallas_call x1, Pallas kernels, on_device(): pl.pallas_call(kernel, out_shape=jax.ShapeDtypeStruct(cross_kernel.shape,...  47.9 us

profile of v6, /device:TPU:23, one launch (start us, length us, event | category | flops | bytes accessed | tf_op | source)
XLA Modules:
  0.0 48.7 jit_solution(17601904389379001127)
XLA Ops:
  0.0 47.9 %shard_map.37 = f32[1024,128]{1,0:T(8,128)S(1)} custom-call(f32[1024,128]{1,0:T(8,128)} %b_hbm.1, f32[2,64,1024]{2,1,0:T(8,128)} %f_hbm.1, f32[2,64,512]{2,1,0:T(8,128)} %inv_hbm.1), custom_call_target="tpu_custom_call" | custom-call | tf_op jit(solution)/shard_map/pallas_call | solution.py:357
  47.9 0.8 %copy.5 = f32[1024,128]{1,0:T(8,128)} copy(f32[1024,128]{1,0:T(8,128)S(1)} %shard_map.37) | data formatting | bytes 1048576
